TPU v7x, 32 devices: a whole 2x2x4 slice. The times are simulated.
32 devices in a mesh: ctx: 8 (over z, core), exp: 4 (over y, x).
Axes of the slice: x: 2, y: 2, z: 4, core: 2. Of those that a mesh axis runs over, the one named last changes fastest.
Arguments:
- queries: bfloat16 [4, 1024, 8192], P('exp', 'ctx'), may hold values from -64 to 64
- key_head_vectors: bfloat16 [4, 1024, 512], P('exp', 'ctx'), may hold values from -6 to 6
- value_head_vectors: bfloat16 [4, 1024, 512], P('exp', 'ctx'), may hold values from -6 to 6
- segment_ids: int32 [4, 1024], P('exp', 'ctx'), may hold values from 0 to 3, never falling along the last dimension, each value on 1 to 512 neighbouring positions
- normed: bfloat16 [4, 1024, 4096], P('exp', 'ctx'), may hold values from -6 to 6
- expert_ids: int32 [4, 1024, 2], P('exp', 'ctx'), may hold values from 0 to 3, all different within a row; in each aligned block of 128 rows (0 to 127, 128 to 255, ..., all dimensions but the last counted through in order) at most 80 rows name the same one
- gate_probs: float32 [4, 1024, 2], P('exp', 'ctx'), may hold values from 0.1 to 1
- gate_weight: bfloat16 [4, 768, 4096], P('exp', 'ctx'), may hold values from -0.09375 to 0.09375
- up_weight: bfloat16 [4, 768, 4096], P('exp', 'ctx'), may hold values from -0.09375 to 0.09375
- down_weight: bfloat16 [4, 768, 4096], P('exp', 'ctx'), may hold values from -0.21875 to 0.21875
Outputs:
- context: bfloat16 [4, 1024, 8192], P('exp', 'ctx')
- expert_mix: bfloat16 [4, 1024, 4096], P('exp', 'ctx')
Inputs may be any that keep to these rules, and one draw needn't show every extreme that they name: `segment_ids`: ids never fall along a sequence; an even id marks a document, an odd id the question that reads the document just before it; each segment holds at most 512 positions and one holds exactly that many. `expert_ids`: each position names 2 different experts. Within the rows of one device no expert is named more than 80 times, a bound that some block reaches.
All inputs are finite; a program needn't handle non-finite values.
Results may differ from a plain program's by a relative error of at most 0.0058.
Values may be sent and summed in bfloat16 or wider, within the bound.
A program may use at most 128 MiB of HBM per device.

v0:
```python
import jax
import jax.numpy as jnp
from jax import lax
from jax.sharding import PartitionSpec as P

QUERY_HEAD_COUNT = 64
KEY_HEAD_COUNT = 4
HEAD_SIZE = 128


def attend_mask(query_places, key_places, query_segments, key_segments):
    causal = key_places[None, :] <= query_places[:, None]
    same_segment = key_segments[None, :] == query_segments[:, None]
    source = (query_segments[:, None] % 2 == 1) & (
        key_segments[None, :] == query_segments[:, None] - 1
    )
    return causal & (same_segment | source)


def softmax_rows(scores, allowed):
    masked = jnp.where(allowed[None], scores, -1e30)
    row_peak = jnp.max(masked, axis=-1, keepdims=True)
    exponent = jnp.where(allowed[None], jnp.exp(masked - row_peak), 0.0)
    row_total = jnp.sum(exponent, axis=-1, keepdims=True)
    return (exponent / row_total).astype(jnp.bfloat16)


def context_by_keys(query_rows, key_token_rows, value_token_rows, segment_row):
    shard_tokens = query_rows.shape[0]
    key_all, value_all, segment_all = (
        lax.all_gather(key_token_rows, "ctx", axis=0, tiled=True),
        lax.all_gather(value_token_rows, "ctx", axis=0, tiled=True),
        lax.all_gather(segment_row.astype(jnp.bfloat16), "ctx", axis=0, tiled=True),
    )
    span_length = key_all.shape[0]
    query_group_count = QUERY_HEAD_COUNT // KEY_HEAD_COUNT
    query_head_rows = query_rows.reshape(
        shard_tokens, KEY_HEAD_COUNT, query_group_count, HEAD_SIZE
    ).transpose(1, 2, 0, 3)
    key_head_rows = key_all.reshape(span_length, KEY_HEAD_COUNT, HEAD_SIZE).transpose(1, 0, 2)
    value_head_rows = value_all.reshape(span_length, KEY_HEAD_COUNT, HEAD_SIZE).transpose(1, 0, 2)
    segments = segment_all.astype(jnp.int32)
    query_places = lax.axis_index("ctx") * shard_tokens + jnp.arange(shard_tokens, dtype=jnp.int32)
    allowed = attend_mask(
        query_places, jnp.arange(span_length, dtype=jnp.int32), segment_row, segments
    )

    def per_head(operands):
        query_block, key_block, value_block = operands
        scores = jnp.einsum(
            "gqd,kd->gqk", query_block, key_block, preferred_element_type=jnp.float32
        ) * HEAD_SIZE ** (-0.5)
        weights = softmax_rows(scores, allowed)
        return jnp.einsum(
            "gqk,kd->gqd", weights, value_block, preferred_element_type=jnp.float32
        ).astype(jnp.bfloat16)

    heads_out = lax.map(per_head, (query_head_rows, key_head_rows, value_head_rows))
    return heads_out.transpose(2, 0, 1, 3).reshape(shard_tokens, QUERY_HEAD_COUNT * HEAD_SIZE)


def route_experts(normed, expert_ids, gate_probs, gate_weight, up_weight, down_weight):
    shard_tokens = normed.shape[1]
    model_width = normed.shape[2]
    per_token = expert_ids.shape[2]
    experts = lax.axis_size("exp")
    capacity = shard_tokens * per_token * 5 // (4 * experts)
    tokens = normed.reshape(shard_tokens, model_width)
    flat_ids = expert_ids.reshape(shard_tokens * per_token)
    onehot = (flat_ids[:, None] == jnp.arange(experts, dtype=jnp.int32)[None, :]).astype(jnp.int32)
    bucket_rank = jnp.sum((jnp.cumsum(onehot, axis=0) - onehot) * onehot, axis=1)
    targets = flat_ids * capacity + bucket_rank
    owners = jnp.arange(shard_tokens * per_token, dtype=jnp.int32) // per_token
    sources = jnp.zeros((experts * capacity,), jnp.int32).at[targets].set(owners)
    outgoing = tokens[sources].reshape(experts, capacity, model_width)
    incoming = lax.all_to_all(outgoing, "exp", split_axis=0, concat_axis=0, tiled=True)
    inputs = incoming.reshape(experts * capacity, model_width)
    gate_piece = lax.all_gather(gate_weight[0], "ctx", axis=0, tiled=True)
    up_piece = lax.all_gather(up_weight[0], "ctx", axis=0, tiled=True)
    down_piece = lax.all_gather(down_weight[0], "ctx", axis=0, tiled=True)
    gate_part = lax.dot_general(
        inputs, gate_piece, (((1,), (1,)), ((), ())), preferred_element_type=jnp.float32
    )
    up_part = lax.dot_general(
        inputs, up_piece, (((1,), (1,)), ((), ())), preferred_element_type=jnp.float32
    )
    activation = (jax.nn.silu(gate_part) * up_part).astype(jnp.bfloat16)
    results = jnp.dot(activation, down_piece, preferred_element_type=jnp.float32)
    returned = lax.all_to_all(
        results.astype(jnp.bfloat16).reshape(experts, capacity, model_width),
        "exp",
        split_axis=0,
        concat_axis=0,
        tiled=True,
    )
    picked = returned.reshape(experts * capacity, model_width)[targets].reshape(
        shard_tokens, per_token, model_width
    )
    mixture = jnp.sum(
        gate_probs.reshape(shard_tokens, per_token, 1) * picked.astype(jnp.float32), axis=1
    )
    return mixture.astype(jnp.bfloat16)


def on_device(
    queries,
    key_head_vectors,
    value_head_vectors,
    segment_ids,
    normed,
    expert_ids,
    gate_probs,
    gate_weight,
    up_weight,
    down_weight,
):
    shard_tokens = queries.shape[1]
    query_rows = queries.reshape(shard_tokens, QUERY_HEAD_COUNT * HEAD_SIZE)
    key_token_rows = key_head_vectors.reshape(shard_tokens, KEY_HEAD_COUNT * HEAD_SIZE)
    value_token_rows = value_head_vectors.reshape(shard_tokens, KEY_HEAD_COUNT * HEAD_SIZE)
    segment_row = segment_ids.reshape(shard_tokens)
    context = context_by_keys(query_rows, key_token_rows, value_token_rows, segment_row)
    mixture = route_experts(normed, expert_ids, gate_probs, gate_weight, up_weight, down_weight)
    return (
        context.reshape(1, shard_tokens, QUERY_HEAD_COUNT * HEAD_SIZE),
        mixture.reshape(1, shard_tokens, normed.shape[2]),
    )


def solution(mesh):
    in_specs = (
        P("exp", "ctx", None),
        P("exp", "ctx", None),
        P("exp", "ctx", None),
        P("exp", "ctx"),
        P("exp", "ctx", None),
        P("exp", "ctx", None),
        P("exp", "ctx", None),
        P("exp", "ctx", None),
        P("exp", "ctx", None),
        P("exp", "ctx", None),
    )
    out_specs = (P("exp", "ctx", None), P("exp", "ctx", None))
    return jax.shard_map(
        on_device, mesh=mesh, in_specs=in_specs, out_specs=out_specs, check_vma=False
    )
```

profile of v0, /device:TPU:0, one launch (start us, length us, event | category | flops | bytes accessed | tf_op | source)
XLA Modules:
  0.0 341.3 jit_solution(3326753072393988957)
XLA Ops:
  16.2 3.9 %gather_fusion = bf16[320,4096]{1,0:T(8,128)(2,1)} fusion(bf16[128,4096]{1,0:T(8,128)(2,1)S(1)} %bitcast.112, s32[1024]{0:T(1024)S(1)} %pad_clamp_fusion.1), kind=kCustom, calls=%fused_computation | custom fusion | bytes 5244160 | tf_op jit(solution)/shard_map/gather | solution.py:75
  20.1 5.4 %all-to-all-start = ((bf16[4,80,4096]{2,1,0:T(8,128)(2,1)}), bf16[4,80,4096]{2,1,0:T(8,128)(2,1)}, u32[]{:S(2)}, u32[]{:S(2)}) async-start(bf16[4,80,4096]{2,1,0:T(8,128)(2,1)} %bitcast.113), calls=%async_computation | async-start | bytes 5242880 | tf_op jit(solution)/shard_map/all_to_all | solution.py:76
  29.0 13.1 %all-gather.5 = bf16[8,1,128]{2,1,0:T(2,128)(2,1)S(1)} all-gather(bf16[1,1,128]{2,1,0:T(2,128)(2,1)S(1)} %convert_bitcast_fusion.1), channel_id=1, replica_groups=mesh['ctx'=8,'exp'=4] {'ctx'}, dimensions={0}, use_global_device_ids=true | all-gather | bytes 2304 | tf_op jit(solution)/shard_map/all_gather | solution.py:33
  42.1 14.9 %all-to-all-done = bf16[4,80,4096]{2,1,0:T(8,128)(2,1)} async-done(((bf16[4,80,4096]{2,1,0:T(8,128)(2,1)}), bf16[4,80,4096]{2,1,0:T(8,128)(2,1)}, u32[]{:S(2)}, u32[]{:S(2)}) %all-to-all-start) | async-done | bytes 2621472 | tf_op jit(solution)/shard_map/all_to_all | solution.py:76
  57.0 20.2 %all-gather.16.cloned.1.call-done = bf16[1,768,4096]{2,1,0:T(8,128)(2,1)} async-done(((bf16[1,96,4096]{2,1,0:T(8,128)(2,1)}), bf16[1,768,4096]{2,1,0:T(8,128)(2,1)}) %all-gather.16.cloned.1.call-update) | async-done | bytes 6291472 | tf_op jit(solution)/shard_map/all_gather | solution.py:78
  77.1 5.8 %fusion.46 = f32[320,768]{1,0:T(8,128)S(1)} fusion(bf16[320,4096]{1,0:T(8,128)(2,1)} %bitcast.17, bf16[1,768,4096]{2,1,0:T(8,128)(2,1)} %all-gather.16.cloned.1.call-done), kind=kOutput, calls=%fused_computation.39 | convolution fusion | flops 2013265920 | bytes 9895936 | tf_op jit(solution)/shard_map/dot_general | solution.py:81
  83.0 59.4 %all-gather.18.cloned.1.call-done = bf16[1,768,4096]{2,1,0:T(8,128)(2,1)} async-done(((bf16[1,96,4096]{2,1,0:T(8,128)(2,1)}), bf16[1,768,4096]{2,1,0:T(8,128)(2,1)}) %all-gather.18.cloned.1.call-update) | async-done | bytes 6291472 | tf_op jit(solution)/shard_map/all_gather | solution.py:79
  142.3 65.1 %all-gather.20.cloned.1.call-done = bf16[1,768,4096]{2,1,0:T(8,128)(2,1)} async-done(((bf16[1,96,4096]{2,1,0:T(8,128)(2,1)}), bf16[1,768,4096]{2,1,0:T(8,128)(2,1)}) %all-gather.20.cloned.1.call-update) | async-done | bytes 6291472 | tf_op jit(solution)/shard_map/all_gather | solution.py:80
  207.4 12.5 %fusion.48 = bf16[320,4096]{1,0:T(8,128)(2,1)} fusion(bf16[1,768,4096]{2,1,0:T(8,128)(2,1)} %all-gather.20.cloned.1.call-done, bf16[320,4096]{1,0:T(8,128)(2,1)} %bitcast.17, bf16[1,768,4096]{2,1,0:T(8,128)(2,1)} %all-gather.18.cloned.1.call-done, f32[320,768]{1,0:T(8,128)S(1)} %fusion.46), kind=kOutput, calls=%fused_computation.41 | convolution fusion | flops 4029317120 | bytes 18808832 | tf_op jit(solution)/shard_map/dot_general | solution.py:88
  219.9 4.9 %all-to-all-start.1 = ((bf16[4,80,4096]{2,1,0:T(8,128)(2,1)}), bf16[4,80,4096]{2,1,0:T(8,128)(2,1)}, u32[]{:S(2)}, u32[]{:S(2)}) async-start(bf16[4,80,4096]{2,1,0:T(8,128)(2,1)} %bitcast.114), calls=%async_computation.1 | async-start | bytes 5242880 | tf_op jit(solution)/shard_map/all_to_all | solution.py:89
  224.8 7.3 %all-gather.12.cloned.1.call-done = bf16[1,1024,512]{1,2,0:T(8,128)(2,1)} async-done(((bf16[1,128,512]{1,2,0:T(8,128)(2,1)}), bf16[1,1024,512]{1,2,0:T(8,128)(2,1)}) %all-gather.12.cloned.1.call-update) | async-done | bytes 1048592 | tf_op jit(solution)/shard_map/all_gather | solution.py:31
  232.1 24.0 %all-gather.14.cloned.1.call-done = bf16[1,1024,512]{1,2,0:T(8,128)(2,1)} async-done(((bf16[1,128,512]{1,2,0:T(8,128)(2,1)}), bf16[1,1024,512]{1,2,0:T(8,128)(2,1)}) %all-gather.14.cloned.1.call-update) | async-done | bytes 1048592 | tf_op jit(solution)/shard_map/all_gather | solution.py:32
  256.1 52.5 %while.11 = (s32[]{:T(128)}, bf16[4,16,128,128]{3,2,1,0:T(8,128)(2,1)S(1)}, bf16[4,16,128,128]{2,3,1,0:T(8,128)(2,1)}, bf16[4,1024,128]{1,2,0:T(8,128)(2,1)}, bf...) while((s32[]{:T(128)}, ...), condition=%wide.region_3.4_spmd.clone, body=%wide.region_0.3_spmd.clone.sunk | while | flops 1089471488 | bytes 18767596 | solution.py:58
  256.4 7.9 %fusion.89 = (f32[16,128]{1,0:T(8,128)S(1)}, f32[16,128,1024]{2,1,0:T(8,128)}) fusion(pred[128,1024]{1,0:T(8,128)(4,1)S(1)} %fusion.88, bf16[4,16,128,128]{2,3,1,0:T(8,128)(2,1)} %get-tuple-element.195, s32[]{:T(128)} %get-tuple-element.182, bf16[4,1024,128]{1,2,0:T(8,128)(2,1)} %get-tuple-element.196), kind=kOutput, calls=%fused_computation.74.clone.1 | convolution fusion | flops 547357696 | bytes 9446400 | tf_op jit(solution)/shard_map/while/body/eval_jaxpr/sub | solution.py:23
  264.3 4.9 %fusion.90 = bf16[4,16,128,128]{3,2,1,0:T(8,128)(2,1)S(1)} fusion(bf16[4,16,128,128]{3,2,1,0:T(8,128)(2,1)S(1)} %get-tuple-element.183, s32[]{:T(128)} %get-tuple-element.182, f32[16,128,1024]{2,1,0:T(8,128)} %get-tuple-element.169, f32[16,128]{1,0:T(8,128)S(1)} %get-tuple-element.170, bf16[4,1024,128]{1,2,0:T(8,128)(2,1)} %get-tuple-element.197), kind=kOutput, calls=%fused_computation.15.clone.1 | convolution fusion | flops 541327360 | bytes 9184256 | tf_op jit(solution)/shard_map/while/body/eval_jaxpr/gqk,kd->gqd/dot_general | solution.py:54
  269.5 7.9 %fusion.89 = (f32[16,128]{1,0:T(8,128)S(1)}, f32[16,128,1024]{2,1,0:T(8,128)}) fusion(pred[128,1024]{1,0:T(8,128)(4,1)S(1)} %fusion.88, bf16[4,16,128,128]{2,3,1,0:T(8,128)(2,1)} %get-tuple-element.195, s32[]{:T(128)} %get-tuple-element.182, bf16[4,1024,128]{1,2,0:T(8,128)(2,1)} %get-tuple-element.196), kind=kOutput, calls=%fused_computation.74.clone.1 | convolution fusion | flops 547357696 | bytes 9446400 | tf_op jit(solution)/shard_map/while/body/eval_jaxpr/sub | solution.py:23
  277.5 4.9 %fusion.90 = bf16[4,16,128,128]{3,2,1,0:T(8,128)(2,1)S(1)} fusion(bf16[4,16,128,128]{3,2,1,0:T(8,128)(2,1)S(1)} %get-tuple-element.183, s32[]{:T(128)} %get-tuple-element.182, f32[16,128,1024]{2,1,0:T(8,128)} %get-tuple-element.169, f32[16,128]{1,0:T(8,128)S(1)} %get-tuple-element.170, bf16[4,1024,128]{1,2,0:T(8,128)(2,1)} %get-tuple-element.197), kind=kOutput, calls=%fused_computation.15.clone.1 | convolution fusion | flops 541327360 | bytes 9184256 | tf_op jit(solution)/shard_map/while/body/eval_jaxpr/gqk,kd->gqd/dot_general | solution.py:54
  282.7 7.9 %fusion.89 = (f32[16,128]{1,0:T(8,128)S(1)}, f32[16,128,1024]{2,1,0:T(8,128)}) fusion(pred[128,1024]{1,0:T(8,128)(4,1)S(1)} %fusion.88, bf16[4,16,128,128]{2,3,1,0:T(8,128)(2,1)} %get-tuple-element.195, s32[]{:T(128)} %get-tuple-element.182, bf16[4,1024,128]{1,2,0:T(8,128)(2,1)} %get-tuple-element.196), kind=kOutput, calls=%fused_computation.74.clone.1 | convolution fusion | flops 547357696 | bytes 9446400 | tf_op jit(solution)/shard_map/while/body/eval_jaxpr/sub | solution.py:23
  290.6 4.9 %fusion.90 = bf16[4,16,128,128]{3,2,1,0:T(8,128)(2,1)S(1)} fusion(bf16[4,16,128,128]{3,2,1,0:T(8,128)(2,1)S(1)} %get-tuple-element.183, s32[]{:T(128)} %get-tuple-element.182, f32[16,128,1024]{2,1,0:T(8,128)} %get-tuple-element.169, f32[16,128]{1,0:T(8,128)S(1)} %get-tuple-element.170, bf16[4,1024,128]{1,2,0:T(8,128)(2,1)} %get-tuple-element.197), kind=kOutput, calls=%fused_computation.15.clone.1 | convolution fusion | flops 541327360 | bytes 9184256 | tf_op jit(solution)/shard_map/while/body/eval_jaxpr/gqk,kd->gqd/dot_general | solution.py:54
  295.8 7.9 %fusion.89 = (f32[16,128]{1,0:T(8,128)S(1)}, f32[16,128,1024]{2,1,0:T(8,128)}) fusion(pred[128,1024]{1,0:T(8,128)(4,1)S(1)} %fusion.88, bf16[4,16,128,128]{2,3,1,0:T(8,128)(2,1)} %get-tuple-element.195, s32[]{:T(128)} %get-tuple-element.182, bf16[4,1024,128]{1,2,0:T(8,128)(2,1)} %get-tuple-element.196), kind=kOutput, calls=%fused_computation.74.clone.1 | convolution fusion | flops 547357696 | bytes 9446400 | tf_op jit(solution)/shard_map/while/body/eval_jaxpr/sub | solution.py:23
  303.7 4.9 %fusion.90 = bf16[4,16,128,128]{3,2,1,0:T(8,128)(2,1)S(1)} fusion(bf16[4,16,128,128]{3,2,1,0:T(8,128)(2,1)S(1)} %get-tuple-element.183, s32[]{:T(128)} %get-tuple-element.182, f32[16,128,1024]{2,1,0:T(8,128)} %get-tuple-element.169, f32[16,128]{1,0:T(8,128)S(1)} %get-tuple-element.170, bf16[4,1024,128]{1,2,0:T(8,128)(2,1)} %get-tuple-element.197), kind=kOutput, calls=%fused_computation.15.clone.1 | convolution fusion | flops 541327360 | bytes 9184256 | tf_op jit(solution)/shard_map/while/body/eval_jaxpr/gqk,kd->gqd/dot_general | solution.py:54
  315.2 6.0 %gather_fusion.1 = bf16[256,4096]{1,0:T(8,128)(2,1)S(1)} fusion(bf16[320,4096]{1,0:T(8,128)(2,1)} %bitcast.22, s32[1024]{0:T(1024)S(1)} %pad_clamp_fusion), kind=kCustom, calls=%fused_computation.1 | custom fusion | bytes 4195328 | tf_op jit(solution)/shard_map/gather | solution.py:96
  321.2 4.0 %reshape.151 = f32[128,2,4096]{2,1,0:T(2,128)} reshape(bf16[256,4096]{1,0:T(8,128)(2,1)S(1)} %gather_fusion.1) | data formatting | bytes 6291456 | tf_op jit(solution)/shard_map/convert_element_type | solution.py:100
  325.2 9.6 %multiply_reduce_fusion = bf16[128,4096]{1,0:T(8,128)(2,1)} fusion(f32[128,2,4096]{2,1,0:T(2,128)} %reshape.151, f32[128,2]{1,0:T(8,128)S(1)} %copy.36), kind=kLoop, calls=%fused_computation.42 | loop fusion | flops 1572864 | bytes 5243904 | tf_op jit(solution)/shard_map/reduce_sum | solution.py:99
  (61 shorter events, 20.0 us)
Async XLA Ops:
  7.2 9.1 %copy-start = (bf16[1,128,4096]{2,1,0:T(8,128)(2,1)S(1)}, bf16[1,128,4096]{2,1,0:T(8,128)(2,1)}, u32[]{:S(2)}) copy-start(bf16[1,128,4096]{2,1,0:T(8,128)(2,1)} %param.16) | copy-start | bytes 3145732
  7.2 70.0 %all-gather.16.cloned.1.call-start = ((), (), s32[]{:S(2)}) async-start(), calls=%async_computation.4 | async-start | bytes 7077888 | tf_op jit(solution)/shard_map/all_gather | solution.py:78
  7.9 134.4 %all-gather.18.cloned.1.call-start = ((), (), s32[]{:S(2)}) async-start(), calls=%async_computation.5 | async-start | bytes 7077888 | tf_op jit(solution)/shard_map/all_gather | solution.py:79
  8.7 198.7 %all-gather.20.cloned.1.call-start = ((), (), s32[]{:S(2)}) async-start(), calls=%async_computation.6 | async-start | bytes 7077888 | tf_op jit(solution)/shard_map/all_gather | solution.py:80
  9.4 222.7 %all-gather.12.cloned.1.call-start = ((), (), s32[]{:S(2)}) async-start(), calls=%async_computation.2 | async-start | bytes 1179648 | tf_op jit(solution)/shard_map/all_gather | solution.py:31
  20.1 5.5 %copy-start.4 = (bf16[1,128,512]{2,1,0:T(8,128)(2,1)S(1)}, bf16[1,128,512]{2,1,0:T(8,128)(2,1)}, u32[]{:S(2)}) copy-start(bf16[1,128,512]{2,1,0:T(8,128)(2,1)} %param.14) | copy-start | bytes 393220
  20.1 6.2 %copy-start.6 = (f32[1,128,2]{1,2,0:T(2,128)S(1)}, f32[1,128,2]{1,2,0:T(2,128)}, u32[]{:S(2)}) copy-start(f32[1,128,2]{1,2,0:T(2,128)} %param.18) | copy-start | bytes 3076
  20.1 6.4 %copy-start.1 = (bf16[1,128,8192]{2,1,0:T(8,128)(2,1)S(1)}, bf16[1,128,8192]{2,1,0:T(8,128)(2,1)}, u32[]{:S(2)}) copy-start(bf16[1,128,8192]{2,1,0:T(8,128)(2,1)} %param.12) | copy-start | bytes 6291460
  20.1 8.9 %copy-start.5 = (s32[1,128]{1,0:T(1,128)S(1)}, s32[1,128]{1,0:T(1,128)}, u32[]{:S(2)}) copy-start(s32[1,128]{1,0:T(1,128)} %param.15) | copy-start | bytes 1540
  20.1 36.9 %all-to-all-start = ((bf16[4,80,4096]{2,1,0:T(8,128)(2,1)}), bf16[4,80,4096]{2,1,0:T(8,128)(2,1)}, u32[]{:S(2)}, u32[]{:S(2)}) async-start(bf16[4,80,4096]{2,1,0:T(8,128)(2,1)} %bitcast.113), calls=%async_computation | async-start | bytes 5242880 | tf_op jit(solution)/shard_map/all_to_all | solution.py:76
  25.5 230.6 %all-gather.14.cloned.1.call-start = ((), (), s32[]{:S(2)}) async-start(), calls=%async_computation.3 | async-start | bytes 1179648 | tf_op jit(solution)/shard_map/all_gather | solution.py:32
  219.9 36.2 %copy-start.2 = (bf16[4,16,128,128]{3,2,1,0:T(8,128)(2,1)S(1)}, bf16[4,16,128,128]{3,2,1,0:T(8,128)(2,1)}, u32[]{:S(2)}) copy-start(bf16[4,16,128,128]{3,2,1,0:T(8,128)(2,1)} %custom-call.4) | copy-start | bytes 6291460
  219.9 95.3 %all-to-all-start.1 = ((bf16[4,80,4096]{2,1,0:T(8,128)(2,1)}), bf16[4,80,4096]{2,1,0:T(8,128)(2,1)}, u32[]{:S(2)}, u32[]{:S(2)}) async-start(bf16[4,80,4096]{2,1,0:T(8,128)(2,1)} %bitcast.114), calls=%async_computation.1 | async-start | bytes 5242880 | tf_op jit(solution)/shard_map/all_to_all | solution.py:89
  308.6 1.3 copy-start.3
Sparse Core Ops, SparseCore 0:
  9.7 67.4 all-gather.15
  78.8 63.4 all-gather.17
  144.0 63.3 all-gather.19
  209.4 22.6 all-gather.11
  233.5 22.5 all-gather.13
where the time goes:
time: 342 us; the launch traced here: 341 us
  waiting for transfers between devices  193 us (56%)
  matrix products  69.6 us (20%)
  local copies, waits for them, and re-layouts  28.4 us (8%)
  between operations  13.9 us (4%)
  blocking collectives  13.1 us (4%)
  other arithmetic  12.8 us (4%)
  starting transfers between devices  10.5 us (3%)
    all_gather x1, waiting for transfers between devices, route_experts(): down_piece = lax.all_gather(down_weight[0], 'ctx', axis=0, tiled=True)  65.1 us
    all_gather x1, waiting for transfers between devices, route_experts(): up_piece = lax.all_gather(up_weight[0], 'ctx', axis=0, tiled=True)  59.4 us
    sub x4, matrix products, softmax_rows(): exponent = jnp.where(allowed[None], jnp.exp(masked - row_peak), 0.0)  31.8 us
    all_gather x1, waiting for transfers between devices, context_by_keys(): lax.all_gather(value_token_rows, 'ctx', axis=0, tiled=True)  24 us
    all_gather x1, waiting for transfers between devices, route_experts(): gate_piece = lax.all_gather(gate_weight[0], 'ctx', axis=0, tiled=True)  20.2 us
    dot_general x4, matrix products, per_head(): jnp.einsum('gqk,kd->gqd', weights, value_block, preferred_element_type=jn...  19.6 us
    all_to_all x1, waiting for transfers between devices, route_experts(): lax.all_to_all(outgoing, 'exp', split_axis=0, concat_axis=0, tiled=True)  14.9 us
    all_gather x1, blocking collectives, context_by_keys(): lax.all_gather(segment_row.astype(jnp.bfloat16), 'ctx', axis=0, tiled=True)  13.1 us
  transfers between devices with their start and end apart: 7, of which 6 were waited for; matrix products, arithmetic and copies ran while one was open for 26% of the time, Pallas kernels for 0%

commit v1 on v0

v1 whole, which is shorter than its diff:
```python
import functools
import math

import jax
import jax.numpy as jnp
from jax import lax
from jax.experimental import pallas as pl
from jax.experimental.pallas import tpu as pltpu
from jax.sharding import PartitionSpec as P

KEY_HEAD_COUNT = 4
HEAD_SIZE = 128
COLUMN_BLOCKS = 4
HEADS_AT_ONCE = 4
MESH = pl.DeviceIdType.MESH
F32 = jnp.float32
BF16 = jnp.bfloat16


def kernel(
    n_ctx, n_exp, cap,
    q_hbm, k_hbm, v_hbm, seg_in, x_in, ids_in, prob_in, gate_hbm, up_hbm, down_hbm,
    ctx_out, mix_out,
    q_buf, k_buf, v_buf, seg_buf, bias, ctx_buf, weights, rows_out, rows_in,
    total, result, returned, pick, gates, mix_buf,
    local_sem, kv_send, kv_swap, kv_recv, w_left, w_right, w_swap, w_recv,
    x_send, x_recv, r_send, r_recv, out_sem,
):
    me = lax.axis_index("ctx")
    mine = lax.axis_index("exp")
    n_z = n_ctx // 2
    z, core = me // 2, me % 2
    mate = me + 1 - 2 * core
    tokens, width = x_in.shape
    group = q_buf.shape[1] // (KEY_HEAD_COUNT * HEAD_SIZE)
    span = n_ctx * tokens

    def send(src, dst, send_sem, recv_sem, where):
        return pltpu.make_async_remote_copy(
            src_ref=src, dst_ref=dst, send_sem=send_sem, recv_sem=recv_sem,
            device_id=where, device_id_type=MESH,
        )

    def key_rows(slot):
        return pl.ds(pl.multiple_of(slot * tokens, tokens), tokens)

    own_weights = (gate_hbm, up_hbm, down_hbm)
    own_kv = (k_hbm, v_hbm, seg_in)

    def kv_slot(j, slot):
        return seg_buf.at[slot] if j == 2 else (k_buf, v_buf)[j].at[key_rows(slot)]

    barrier = pltpu.get_barrier_semaphore()
    for d in range(1, n_z):
        pl.semaphore_signal(barrier, inc=1, device_id={"ctx": (z + d) % n_z * 2 + core}, device_id_type=MESH)
    pl.semaphore_signal(barrier, inc=1, device_id={"ctx": mate}, device_id_type=MESH)
    for d in range(1, n_exp):
        pl.semaphore_signal(barrier, inc=1, device_id={"exp": (mine + d) % n_exp}, device_id_type=MESH)
    pl.semaphore_wait(barrier, n_z - 1 + 1 + n_exp - 1)

    def kv_out(d, j):
        there = (z + d) % n_z
        return send(own_kv[j], kv_slot(j, me), kv_send.at[there, j], kv_recv.at[me, j], {"ctx": there * 2 + core})

    def kv_pass(d, j):
        slot = (z + d) % n_z * 2 + core
        src = own_kv[j] if d == 0 else kv_slot(j, slot)
        return send(src, kv_slot(j, slot), kv_swap.at[slot // 2, j], kv_recv.at[slot, j], {"ctx": mate})

    for d in range(1, n_z):
        for j in range(3):
            kv_out(d, j).start()
    for j in range(3):
        kv_pass(0, j).start()

    def w_side(side, src, origin, slot, k):
        step = 2 if side else -2
        sem = w_right if side else w_left
        return send(src, weights.at[k, slot], sem.at[origin, k], w_recv.at[slot, k], {"ctx": me + step})

    def w_mate(src, origin, slot, k):
        return send(src, weights.at[k, slot], w_swap.at[origin, k], w_recv.at[slot, k], {"ctx": mate})

    def has_side(side):
        return z + 1 < n_z if side else z > 0

    for k in range(3):
        for side in (0, 1):
            @pl.when(has_side(side))
            def _():
                w_side(side, own_weights[k], z, me, k).start()
        w_mate(own_weights[k], z, me, k).start()

    local = [pltpu.make_async_copy(own_weights[k], weights.at[k, me], local_sem.at[k]) for k in range(3)]
    local += [pltpu.make_async_copy(own_kv[j], kv_slot(j, me), local_sem.at[3 + j]) for j in range(3)]
    local += [pltpu.make_async_copy(q_hbm, q_buf, local_sem.at[6])]
    for copy in local:
        copy.start()

    t_row = lax.broadcasted_iota(jnp.int32, (tokens, tokens), 0)
    t_col = lax.broadcasted_iota(jnp.int32, (tokens, tokens), 1)

    def as_row(column):
        return jnp.sum(jnp.where(t_row == t_col, column, 0), axis=0, keepdims=True)

    ids = ids_in[...]
    probs = prob_in[...]
    id0, id1 = ids[:, 0:1], ids[:, 1:2]
    e_col = lax.broadcasted_iota(jnp.int32, (tokens, n_exp), 1)
    e_row = lax.broadcasted_iota(jnp.int32, (n_exp, tokens), 0)
    named_col = jnp.where((e_col == id0) | (e_col == id1), 1.0, 0.0).astype(F32)
    named_row = jnp.where((e_row == as_row(id0)) | (e_row == as_row(id1)), 1.0, 0.0).astype(F32)
    before = jnp.where(t_col < t_row, 1.0, 0.0).astype(BF16)
    after = jnp.where(t_row < t_col, 1.0, 0.0).astype(BF16)
    rank_col = jnp.dot(before, named_col.astype(BF16), preferred_element_type=F32)
    rank_row = jnp.dot(named_row.astype(BF16), after, preferred_element_type=F32)
    weight_col = jnp.where(e_col == id0, probs[:, 0:1], 0.0) + jnp.where(e_col == id1, probs[:, 1:2], 0.0)
    place_row = lax.broadcasted_iota(jnp.int32, (cap, tokens), 0).astype(F32)
    place_col = lax.broadcasted_iota(jnp.int32, (tokens, cap), 1).astype(F32)
    x = x_in[...]
    for e in range(n_exp):
        chosen = jnp.where(place_row == rank_row[e : e + 1, :], named_row[e : e + 1, :], 0.0)
        rows_out[e] = jnp.dot(chosen.astype(BF16), x, preferred_element_type=F32).astype(BF16)
        back = jnp.where(place_col == rank_col[:, e : e + 1], named_col[:, e : e + 1], 0.0)
        pick[e] = back.astype(BF16)
        gates[e] = weight_col[:, e : e + 1]

    def x_out(d):
        there = (mine + d) % n_exp
        return send(rows_out.at[there], rows_in.at[mine], x_send.at[there], x_recv.at[mine], {"exp": there})

    def x_arrival(d):
        source = (mine + d) % n_exp
        return send(rows_out.at[source], rows_in.at[source], x_send.at[source], x_recv.at[source], {"exp": source})

    for d in range(1, n_exp):
        x_out(d).start()
    rows_in[mine] = rows_out[mine]

    for d in range(1, n_z):
        for j in range(3):
            kv_pass(d, j).wait_recv()
            kv_pass(d, j).start()

    def kv_from_mate(d, j):
        slot = (z + d) % n_z * 2 + 1 - core
        return send(kv_slot(j, slot), kv_slot(j, slot), kv_swap.at[slot // 2, j], kv_recv.at[slot, j], {"ctx": mate})

    for d in range(n_z):
        for j in range(3):
            kv_from_mate(d, j).wait_recv()
    for copy in local[3:]:
        copy.wait()

    own_segment = jnp.sum(
        jnp.where(t_row == t_col, jnp.broadcast_to(seg_buf[me], (tokens, tokens)), 0), axis=1, keepdims=True
    )
    source_segment = jnp.where(own_segment % 2 == 1, own_segment - 1, own_segment)
    for c in range(n_ctx):
        theirs = seg_buf[c]
        allowed = (t_col + c * tokens <= t_row + me * tokens) & (
            (theirs == own_segment) | (theirs == source_segment)
        )
        bias[:, c * tokens : (c + 1) * tokens] = jnp.where(allowed, 0.0, -1e30)

    def relay(s, k):
        for side in (0, 1):
            origin = z - s if side else z + s
            slot = origin * 2 + core

            @pl.when((origin >= 0) & (origin < n_z))
            def _():
                here = weights.at[k, slot]
                w_mate(here, origin, slot, k).wait_recv()

                @pl.when(has_side(side))
                def _():
                    w_side(side, here, origin, slot, k).start()

                w_mate(here, origin, slot, k).start()

    scale = HEAD_SIZE ** -0.5 * math.log2(math.e)

    def attend(g, carry):
        lanes = pl.ds(pl.multiple_of(g * HEAD_SIZE, HEAD_SIZE), HEAD_SIZE)

        def heads(i, inner):
            for u in range(HEADS_AT_ONCE):
                head = g * group + i * HEADS_AT_ONCE + u
                at = pl.ds(pl.multiple_of(head * HEAD_SIZE, HEAD_SIZE), HEAD_SIZE)
                scores = lax.dot_general(
                    q_buf[:, at], k_buf[:, lanes], (((1,), (1,)), ((), ())), preferred_element_type=F32
                )
                scores = scores * scale + bias[...]
                peak = jnp.max(scores, axis=1, keepdims=True)
                power = jnp.exp2(scores - peak)
                share = 1.0 / jnp.sum(power, axis=1, keepdims=True)
                ctx_buf[:, at] = jnp.dot(
                    (power * share).astype(BF16), v_buf[:, lanes], preferred_element_type=F32
                ).astype(BF16)
            return inner

        lax.fori_loop(0, group // HEADS_AT_ONCE, heads, 0)

        @pl.when(g < 3)
        def _():
            relay(1, g)

        return carry

    lax.fori_loop(0, KEY_HEAD_COUNT, attend, 0)
    ctx_copy = pltpu.make_async_copy(ctx_buf, ctx_out, out_sem.at[0])
    ctx_copy.start()

    for d in range(1, n_exp):
        x_arrival(d).wait_recv()
    for copy in local[:3]:
        copy.wait()
    columns = width // COLUMN_BLOCKS

    def block(cb):
        return pl.ds(pl.multiple_of(cb * columns, columns), columns)

    total[...] = jnp.zeros_like(total)

    def hidden_of(origin):
        other = origin * 2 + 1 - core
        for k in range(3):
            w_mate(weights.at[k, other], origin, other, k).wait_recv()
        inputs = rows_in[...].reshape(n_exp * cap, width)
        both = pl.ds(origin * 2, 2)
        gate_w = weights[0, both].reshape(-1, width)
        up_w = weights[1, both].reshape(-1, width)
        gate = lax.dot_general(inputs, gate_w, (((1,), (1,)), ((), ())), preferred_element_type=F32)
        up = lax.dot_general(inputs, up_w, (((1,), (1,)), ((), ())), preferred_element_type=F32)
        hidden = (gate / (1.0 + jnp.exp(-gate)) * up).astype(BF16)

        def down(cb, carry):
            at = block(cb)
            down_w = weights[2, both, :, at].reshape(-1, columns)
            total[:, at] += jnp.dot(hidden, down_w, preferred_element_type=F32)
            return carry

        lax.fori_loop(0, COLUMN_BLOCKS, down, 0)

    hidden_of(z)

    def far(s, carry):
        @pl.when(s > 1)
        def _():
            for k in range(3):
                relay(s, k)

        def one(side, inner):
            origin = z + s - 2 * s * side

            @pl.when((origin >= 0) & (origin < n_z))
            def _():
                hidden_of(origin)

            return inner

        lax.fori_loop(0, 2, one, 0)
        return carry

    lax.fori_loop(1, n_z, far, 0)

    def r_out(d, cb):
        there = (mine + d) % n_exp
        at = pl.ds(cb * columns, columns)
        return send(
            result.at[there, :, at], returned.at[mine, :, at],
            r_send.at[there, cb], r_recv.at[mine, cb], {"exp": there},
        )

    def r_arrival(d, cb):
        source = (mine + d) % n_exp
        at = pl.ds(cb * columns, columns)
        return send(
            result.at[source, :, at], returned.at[source, :, at],
            r_send.at[source, cb], r_recv.at[source, cb], {"exp": source},
        )

    for cb in range(COLUMN_BLOCKS):
        at = pl.ds(cb * columns, columns)
        result[:, :, at] = total[:, at].astype(BF16).reshape(n_exp, cap, columns)
        for d in range(1, n_exp):
            r_out(d, cb).start()
    for cb in range(COLUMN_BLOCKS):
        at = pl.ds(cb * columns, columns)
        mix = gates[mine] * jnp.dot(pick[mine], result[mine, :, at], preferred_element_type=F32)
        for d in range(1, n_exp):
            r_arrival(d, cb).wait_recv()
            source = (mine + d) % n_exp
            mix += gates[source] * jnp.dot(pick[source], returned[source, :, at], preferred_element_type=F32)
        mix_buf[:, at] = mix.astype(BF16)
    mix_copy = pltpu.make_async_copy(mix_buf, mix_out, out_sem.at[1])
    mix_copy.start()

    for d in range(1, n_z):
        for j in range(3):
            kv_out(d, j).wait_send()
    for d in range(n_z):
        for j in range(3):
            kv_pass(d, j).wait_send()
    for k in range(3):
        for side in (0, 1):
            @pl.when(has_side(side))
            def _():
                w_side(side, own_weights[k], z, me, k).wait_send()
        w_mate(own_weights[k], z, me, k).wait_send()

    def sent(s, carry):
        for k in range(3):
            for side in (0, 1):
                origin = z - s if side else z + s
                slot = origin * 2 + core

                @pl.when((origin >= 0) & (origin < n_z))
                def _():
                    here = weights.at[k, slot]

                    @pl.when(has_side(side))
                    def _():
                        w_side(side, here, origin, slot, k).wait_send()

                    w_mate(here, origin, slot, k).wait_send()
        return carry

    lax.fori_loop(1, n_z, sent, 0)
    for d in range(1, n_exp):
        x_out(d).wait_send()
        for cb in range(COLUMN_BLOCKS):
            r_out(d, cb).wait_send()
    ctx_copy.wait()
    mix_copy.wait()


def on_device(
    n_ctx, n_exp,
    queries, key_head_vectors, value_head_vectors, segment_ids,
    normed, expert_ids, gate_probs, gate_weight, up_weight, down_weight,
):
    tokens, q_width = queries.shape[1:]
    kv_width = key_head_vectors.shape[2]
    width = normed.shape[2]
    hidden = gate_weight.shape[1]
    most = tokens * expert_ids.shape[2] * 5 // (4 * n_exp)
    cap = -(-most // 16) * 16
    span = n_ctx * tokens
    n_z = n_ctx // 2
    dma = pltpu.SemaphoreType.DMA
    hbm = pl.BlockSpec(memory_space=pl.ANY)
    vmem = pl.BlockSpec(memory_space=pltpu.VMEM)
    context, mixture = pl.pallas_call(
        functools.partial(kernel, n_ctx, n_exp, cap),
        out_shape=(
            jax.ShapeDtypeStruct((tokens, q_width), BF16),
            jax.ShapeDtypeStruct((tokens, width), BF16),
        ),
        in_specs=[hbm, hbm, hbm, vmem, vmem, vmem, vmem, hbm, hbm, hbm],
        out_specs=(hbm, hbm),
        scratch_shapes=[
            pltpu.VMEM((tokens, q_width), BF16),
            pltpu.VMEM((span, kv_width), BF16),
            pltpu.VMEM((span, kv_width), BF16),
            pltpu.VMEM((n_ctx, 1, tokens), jnp.int32),
            pltpu.VMEM((tokens, span), F32),
            pltpu.VMEM((tokens, q_width), BF16),
            pltpu.VMEM((3, n_ctx, hidden, width), BF16),
            pltpu.VMEM((n_exp, cap, width), BF16),
            pltpu.VMEM((n_exp, cap, width), BF16),
            pltpu.VMEM((n_exp * cap, width), F32),
            pltpu.VMEM((n_exp, cap, width), BF16),
            pltpu.VMEM((n_exp, cap, width), BF16),
            pltpu.VMEM((n_exp, tokens, cap), BF16),
            pltpu.VMEM((n_exp, tokens, 1), F32),
            pltpu.VMEM((tokens, width), BF16),
            dma((7,)),
            dma((n_z, 3)),
            dma((n_z, 3)),
            dma((n_ctx, 3)),
            dma((n_z, 3)),
            dma((n_z, 3)),
            dma((n_z, 3)),
            dma((n_ctx, 3)),
            dma((n_exp,)),
            dma((n_exp,)),
            dma((n_exp, COLUMN_BLOCKS)),
            dma((n_exp, COLUMN_BLOCKS)),
            dma((2,)),
        ],
        compiler_params=pltpu.CompilerParams(
            collective_id=0, has_side_effects=True, vmem_limit_bytes=60 * 1024 * 1024
        ),
        name="layer",
    )(
        queries[0], key_head_vectors[0], value_head_vectors[0], segment_ids,
        normed[0], expert_ids[0], gate_probs[0], gate_weight[0], up_weight[0], down_weight[0],
    )
    return context[None], mixture[None]


def solution(mesh):
    rows = P("exp", "ctx", None)
    in_specs = (rows, rows, rows, P("exp", "ctx"), rows, rows, rows, rows, rows, rows)
    return jax.shard_map(
        functools.partial(on_device, mesh.shape["ctx"], mesh.shape["exp"]),
        mesh=mesh, in_specs=in_specs, out_specs=(rows, rows), check_vma=False,
    )
```

time: 342 us -> 223 us (0.65)
  Pallas kernels: 0 us -> 215 us
  waiting for transfers between devices: 193 us -> 0 us
  matrix products: 69.6 us -> 0 us
  local copies, waits for them, and re-layouts: 28.4 us -> 6.98 us
  between operations: 13.9 us -> 0.65 us
  blocking collectives: 13.1 us -> 0 us
  other arithmetic: 12.8 us -> 0 us
  starting transfers between devices: 10.5 us -> 0 us
    pallas_call x0 -> x1, Pallas kernels: none -> 215 us  [on_device(): pl.pallas_call(functools.partial(kernel, n_ctx, n_exp, cap), out_shape=(j...]
    all_gather x5 -> x0, waiting for transfers between devices: 176 us -> none  [the longest x1 65.1 us: route_experts(): down_piece = lax.all_gather(down_weight[0], 'ctx', axis=0, tiled=True)]
    dot_general x6 -> x0, matrix products: 37.9 us -> none  [the longest x4 19.6 us: per_head(): jnp.einsum('gqk,kd->gqd', weights, value_block, preferred_element_type=jn...]
    sub x4 -> x0, matrix products: 31.8 us -> none  [softmax_rows(): exponent = jnp.where(allowed[None], jnp.exp(masked - row_peak), 0.0)]
    all_to_all x2 -> x0, waiting for transfers between devices: 14.9 us -> none  [the longest x1 14.9 us: route_experts(): lax.all_to_all(outgoing, 'exp', split_axis=0, concat_axis=0, tiled=True)]
    all_gather x1 -> x0, blocking collectives: 13.1 us -> none  [context_by_keys(): lax.all_gather(segment_row.astype(jnp.bfloat16), 'ctx', axis=0, tiled=True)]
    all_to_all x2 -> x0, starting transfers between devices: 10.3 us -> none  [the longest x1 5.44 us: route_experts(): lax.all_to_all(outgoing, 'exp', split_axis=0, concat_axis=0, tiled=True)]
    gather x2 -> x0, local copies, waits for them, and re-layouts: 9.82 us -> none  [the longest x1 5.96 us: route_experts(): returned.reshape(experts * capacity, model_width)[targets]]
  transfers between devices with their start and end apart: 7 -> 0, of which waited for: 6 -> 0; matrix products, arithmetic and copies ran while one was open for 26% -> 0% of each run, Pallas kernels for 0% -> 0%
where the time goes in v1:
time: 223 us
  Pallas kernels  215 us (96%)
  local copies, waits for them, and re-layouts  6.98 us (3%)
    pallas_call x1, Pallas kernels, on_device(): pl.pallas_call(functools.partial(kernel, n_ctx, n_exp, cap), out_shape=(j...  215 us
    unnamed x6, local copies, waits for them, and re-layouts  6.98 us

profile of v1, /device:TPU:0, one launch (start us, length us, event | category | flops | bytes accessed | tf_op | source)
XLA Modules:
  0.0 222.5 jit_solution(5048990748267794822)
XLA Ops:
  0.6 1.4 copy.12
  2.0 1.4 copy.13
  3.5 214.9 %layer.1 = (bf16[128,8192]{1,0:T(8,128)(2,1)}, bf16[128,4096]{1,0:T(8,128)(2,1)}) custom-call(bf16[128,8192]{1,0:T(8,128)(2,1)} %bitcast.11, bf16[128,512]{1,0:T(8,128)(2,1)} %bitcast.20, bf16[128,512]{1,0:T(8,128)(2,1)} %bitcast.21, s32[1,128]{1,0:T(1,128)} %seg_in.1, bf16[128,4096]{1,0:T(8,128)(2,1)} %bitcast.14, s32[128,2]{1,0:T(8,128)} %bitcast.18, ...), custom_call_target="tpu_custom_call" | custom-call | tf_op jit(solution)/shard_map/layer/pallas_call | solution.py:355
  218.4 0.0 copy-start
  218.4 3.2 %copy.16 = bf16[1,128,8192]{2,1,0:T(8,128)(2,1)} copy(bf16[1,128,8192]{2,1,0:T(8,128)(2,1)} %bitcast.12) | data formatting | bytes 4194304
  221.6 0.0 copy-done
  221.6 1.0 copy.17
Async XLA Ops:
  218.4 3.2 %copy-start = (bf16[128,4096]{1,0:T(8,128)(2,1)S(1)}, bf16[128,4096]{1,0:T(8,128)(2,1)}, u32[]{:S(2)}) copy-start(bf16[128,4096]{1,0:T(8,128)(2,1)} %get-tuple-element.5) | copy-start | bytes 3145732

commit v2 on v1

--- a/solution.py
+++ b/solution.py
@@ -12,6 +12,7 @@
 HEAD_SIZE = 128
 COLUMN_BLOCKS = 4
 HEADS_AT_ONCE = 4
+PIECES = 2 + COLUMN_BLOCKS
 MESH = pl.DeviceIdType.MESH
 F32 = jnp.float32
 BF16 = jnp.bfloat16
@@ -22,7 +23,7 @@
     q_hbm, k_hbm, v_hbm, seg_in, x_in, ids_in, prob_in, gate_hbm, up_hbm, down_hbm,
     ctx_out, mix_out,
     q_buf, k_buf, v_buf, seg_buf, bias, ctx_buf, weights, rows_out, rows_in,
-    total, result, returned, pick, gates, mix_buf,
+    hidden, hidden_all, result, returned, pick, gates, mix_buf,
     local_sem, kv_send, kv_swap, kv_recv, w_left, w_right, w_swap, w_recv,
     x_send, x_recv, r_send, r_recv, out_sem,
 ):
@@ -45,6 +46,17 @@
         return pl.ds(pl.multiple_of(slot * tokens, tokens), tokens)
 
     own_weights = (gate_hbm, up_hbm, down_hbm)
+    columns = width // COLUMN_BLOCKS
+
+    def block(cb):
+        return pl.ds(pl.multiple_of(cb * columns, columns), columns)
+
+    def own_piece(k):
+        return own_weights[k] if k < 2 else down_hbm.at[:, block(k - 2)]
+
+    def piece(k, slot):
+        return weights.at[k, slot] if k < 2 else weights.at[2, slot, :, block(k - 2)]
+
     own_kv = (k_hbm, v_hbm, seg_in)
 
     def kv_slot(j, slot):
@@ -76,20 +88,23 @@
     def w_side(side, src, origin, slot, k):
         step = 2 if side else -2
         sem = w_right if side else w_left
-        return send(src, weights.at[k, slot], sem.at[origin, k], w_recv.at[slot, k], {"ctx": me + step})
+        return send(src, piece(k, slot), sem.at[origin, k], w_recv.at[slot, k], {"ctx": me + step})
 
     def w_mate(src, origin, slot, k):
-        return send(src, weights.at[k, slot], w_swap.at[origin, k], w_recv.at[slot, k], {"ctx": mate})
+        return send(src, piece(k, slot), w_swap.at[origin, k], w_recv.at[slot, k], {"ctx": mate})
 
     def has_side(side):
         return z + 1 < n_z if side else z > 0
 
-    for k in range(3):
+    def share_own(k):
         for side in (0, 1):
             @pl.when(has_side(side))
             def _():
-                w_side(side, own_weights[k], z, me, k).start()
-        w_mate(own_weights[k], z, me, k).start()
+                w_side(side, own_piece(k), z, me, k).start()
+        w_mate(own_piece(k), z, me, k).start()
+
+    for k in range(2):
+        share_own(k)
 
     local = [pltpu.make_async_copy(own_weights[k], weights.at[k, me], local_sem.at[k]) for k in range(3)]
     local += [pltpu.make_async_copy(own_kv[j], kv_slot(j, me), local_sem.at[3 + j]) for j in range(3)]
@@ -170,7 +185,7 @@
 
             @pl.when((origin >= 0) & (origin < n_z))
             def _():
-                here = weights.at[k, slot]
+                here = piece(k, slot)
                 w_mate(here, origin, slot, k).wait_recv()
 
                 @pl.when(has_side(side))
@@ -202,9 +217,10 @@
 
         lax.fori_loop(0, group // HEADS_AT_ONCE, heads, 0)
 
-        @pl.when(g < 3)
-        def _():
-            relay(1, g)
+        for k in range(2):
+            @pl.when(g == 2 * k)
+            def _():
+                relay(1, k)
 
         return carry
 
@@ -216,54 +232,49 @@
         x_arrival(d).wait_recv()
     for copy in local[:3]:
         copy.wait()
-    columns = width // COLUMN_BLOCKS
-
-    def block(cb):
-        return pl.ds(pl.multiple_of(cb * columns, columns), columns)
-
-    total[...] = jnp.zeros_like(total)
 
     def hidden_of(origin):
         other = origin * 2 + 1 - core
-        for k in range(3):
-            w_mate(weights.at[k, other], origin, other, k).wait_recv()
+        for k in range(2):
+            w_mate(piece(k, other), origin, other, k).wait_recv()
         inputs = rows_in[...].reshape(n_exp * cap, width)
         both = pl.ds(origin * 2, 2)
         gate_w = weights[0, both].reshape(-1, width)
         up_w = weights[1, both].reshape(-1, width)
         gate = lax.dot_general(inputs, gate_w, (((1,), (1,)), ((), ())), preferred_element_type=F32)
         up = lax.dot_general(inputs, up_w, (((1,), (1,)), ((), ())), preferred_element_type=F32)
-        hidden = (gate / (1.0 + jnp.exp(-gate)) * up).astype(BF16)
-
-        def down(cb, carry):
-            at = block(cb)
-            down_w = weights[2, both, :, at].reshape(-1, columns)
-            total[:, at] += jnp.dot(hidden, down_w, preferred_element_type=F32)
-            return carry
-
-        lax.fori_loop(0, COLUMN_BLOCKS, down, 0)
+        hidden[origin] = (gate / (1.0 + jnp.exp(-gate)) * up).astype(BF16)
+
+    def both_sides(s, what):
+        def one(side, inner):
+            origin = z + s - 2 * s * side
+
+            @pl.when((origin >= 0) & (origin < n_z))
+            def _():
+                what(origin)
+
+            return inner
+
+        lax.fori_loop(0, 2, one, 0)
 
     hidden_of(z)
 
     def far(s, carry):
+        @pl.when(s == n_z - 1)
+        def _():
+            for k in range(2, PIECES):
+                share_own(k)
+
         @pl.when(s > 1)
         def _():
-            for k in range(3):
+            for k in range(2):
                 relay(s, k)
 
-        def one(side, inner):
-            origin = z + s - 2 * s * side
-
-            @pl.when((origin >= 0) & (origin < n_z))
-            def _():
-                hidden_of(origin)
-
-            return inner
-
-        lax.fori_loop(0, 2, one, 0)
+        both_sides(s, hidden_of)
         return carry
 
     lax.fori_loop(1, n_z, far, 0)
+    hidden_all[...] = jnp.concatenate([hidden[o] for o in range(n_z)], axis=1)
 
     def r_out(d, cb):
         there = (mine + d) % n_exp
@@ -282,8 +293,24 @@
         )
 
     for cb in range(COLUMN_BLOCKS):
+        k = cb + 2
+
+        def pass_on(s, carry):
+            relay(s, k)
+            return carry
+
+        lax.fori_loop(1, n_z, pass_on, 0)
+
+        def from_mate(origin, carry):
+            other = origin * 2 + 1 - core
+            w_mate(piece(k, other), origin, other, k).wait_recv()
+            return carry
+
+        lax.fori_loop(0, n_z, from_mate, 0)
         at = pl.ds(cb * columns, columns)
-        result[:, :, at] = total[:, at].astype(BF16).reshape(n_exp, cap, columns)
+        down_w = weights[2, :, :, at].reshape(-1, columns)
+        out = jnp.dot(hidden_all[...], down_w, preferred_element_type=F32)
+        result[:, :, at] = out.astype(BF16).reshape(n_exp, cap, columns)
         for d in range(1, n_exp):
             r_out(d, cb).start()
     for cb in range(COLUMN_BLOCKS):
@@ -303,22 +330,22 @@
     for d in range(n_z):
         for j in range(3):
             kv_pass(d, j).wait_send()
-    for k in range(3):
+    for k in range(PIECES):
         for side in (0, 1):
             @pl.when(has_side(side))
             def _():
-                w_side(side, own_weights[k], z, me, k).wait_send()
-        w_mate(own_weights[k], z, me, k).wait_send()
+                w_side(side, own_piece(k), z, me, k).wait_send()
+        w_mate(own_piece(k), z, me, k).wait_send()
 
     def sent(s, carry):
-        for k in range(3):
+        for k in range(PIECES):
             for side in (0, 1):
                 origin = z - s if side else z + s
                 slot = origin * 2 + core
 
                 @pl.when((origin >= 0) & (origin < n_z))
                 def _():
-                    here = weights.at[k, slot]
+                    here = piece(k, slot)
 
                     @pl.when(has_side(side))
                     def _():
@@ -370,7 +397,8 @@
             pltpu.VMEM((3, n_ctx, hidden, width), BF16),
             pltpu.VMEM((n_exp, cap, width), BF16),
             pltpu.VMEM((n_exp, cap, width), BF16),
-            pltpu.VMEM((n_exp * cap, width), F32),
+            pltpu.VMEM((n_z, n_exp * cap, 2 * hidden), BF16),
+            pltpu.VMEM((n_exp * cap, n_ctx * hidden), BF16),
             pltpu.VMEM((n_exp, cap, width), BF16),
             pltpu.VMEM((n_exp, cap, width), BF16),
             pltpu.VMEM((n_exp, tokens, cap), BF16),
@@ -380,10 +408,10 @@
             dma((n_z, 3)),
             dma((n_z, 3)),
             dma((n_ctx, 3)),
-            dma((n_z, 3)),
-            dma((n_z, 3)),
-            dma((n_z, 3)),
-            dma((n_ctx, 3)),
+            dma((n_z, PIECES)),
+            dma((n_z, PIECES)),
+            dma((n_z, PIECES)),
+            dma((n_ctx, PIECES)),
             dma((n_exp,)),
             dma((n_exp,)),
             dma((n_exp, COLUMN_BLOCKS)),

time: 223 us -> 199 us (0.89)
  Pallas kernels: 215 us -> 191 us
    pallas_call x1, Pallas kernels: 215 us -> 191 us  [on_device(): pl.pallas_call(functools.partial(kernel, n_ctx, n_exp, cap), out_shape=(j...]
where the time goes in v2:
time: 199 us
  Pallas kernels  191 us (96%)
  local copies, waits for them, and re-layouts  6.98 us (4%)
    pallas_call x1, Pallas kernels, on_device(): pl.pallas_call(functools.partial(kernel, n_ctx, n_exp, cap), out_shape=(j...  191 us
    unnamed x6, local copies, waits for them, and re-layouts  6.98 us

profile of v2, /device:TPU:0, one launch (start us, length us, event | category | flops | bytes accessed | tf_op | source)
XLA Modules:
  0.0 198.8 jit_solution(12959042008692823338)
XLA Ops:
  0.6 1.4 copy.12
  2.0 1.4 copy.13
  3.5 191.1 %layer.1 = (bf16[128,8192]{1,0:T(8,128)(2,1)}, bf16[128,4096]{1,0:T(8,128)(2,1)}) custom-call(bf16[128,8192]{1,0:T(8,128)(2,1)} %bitcast.11, bf16[128,512]{1,0:T(8,128)(2,1)} %bitcast.20, bf16[128,512]{1,0:T(8,128)(2,1)} %bitcast.21, s32[1,128]{1,0:T(1,128)} %seg_in.1, bf16[128,4096]{1,0:T(8,128)(2,1)} %bitcast.14, s32[128,2]{1,0:T(8,128)} %bitcast.18, ...), custom_call_target="tpu_custom_call" | custom-call | tf_op jit(solution)/shard_map/layer/pallas_call | solution.py:382
  194.6 0.0 copy-start
  194.6 3.2 %copy.16 = bf16[1,128,8192]{2,1,0:T(8,128)(2,1)} copy(bf16[1,128,8192]{2,1,0:T(8,128)(2,1)} %bitcast.12) | data formatting | bytes 4194304
  197.8 0.0 copy-done
  197.8 1.0 copy.17
Async XLA Ops:
  194.6 3.2 %copy-start = (bf16[128,4096]{1,0:T(8,128)(2,1)S(1)}, bf16[128,4096]{1,0:T(8,128)(2,1)}, u32[]{:S(2)}) copy-start(bf16[128,4096]{1,0:T(8,128)(2,1)} %get-tuple-element.5) | copy-start | bytes 3145732
